TPU v7x, 128 devices: a whole 4x4x4 slice. The times are simulated.
128 devices in a mesh: guide: 2 (over core), kv: 4 (over y), seq: 16 (over z, x).
Axes of the slice: x: 4, y: 4, z: 4, core: 2. Of those that a mesh axis runs over, the one named last changes fastest.
Arguments:
- hidden: bfloat16 [2, 8, 4608], P(None, None, ('guide', 'seq')), may hold values from -50 to 50
- lengths: int32 [2, 8], replicated, may hold values from 1 to 8192, as said below
- slot_owner: int32 [2, 8], replicated, may hold values from 0 to 7, each once within a row
- allowed_ids: int32 [65536], P(('kv', 'seq')), may hold values from 0 to 131071, as said below
- guidance: float32 [8], replicated, may hold values from 1 to 4
- pre_attn_gain: float32 [4608], P(('guide', 'seq')), may hold values from 0.1 to 1.9
- post_attn_gain: float32 [4608], P(('guide', 'seq')), may hold values from 0.4 to 2.1
- pre_ffw_gain: float32 [4608], P(('guide', 'seq')), may hold values from 0.1 to 1.9
- post_ffw_gain: float32 [4608], P(('guide', 'seq')), may hold values from 0.4 to 2.1
- final_gain: float32 [4608], P(('guide', 'seq')), may hold values from 0.1 to 1.9
- query_weight: bfloat16 [4608, 4096], P(('guide', 'seq'), 'kv'), may hold values from -0.09375 to 0.09375
- key_weight: bfloat16 [4608, 2048], P(('guide', 'seq'), 'kv'), may hold values from -0.09375 to 0.09375
- value_weight: bfloat16 [4608, 2048], P(('guide', 'seq'), 'kv'), may hold values from -0.09375 to 0.09375
- output_weight: bfloat16 [4096, 4608], P('kv', ('guide', 'seq')), may hold values from -1 to 1
- gate_weight: bfloat16 [4608, 36864], P(('guide', 'seq'), 'kv'), may hold values from -1 to 1
- up_weight: bfloat16 [4608, 36864], P(('guide', 'seq'), 'kv'), may hold values from -1 to 1
- down_weight: bfloat16 [36864, 4608], P('kv', ('guide', 'seq')), may hold values from -1 to 1
- embedding: bfloat16 [131072, 4608], P(('kv', 'seq'), 'guide'), may hold values from -1 to 1
- cond_keys: bfloat16 [8, 8192, 2048], P(None, ('guide', 'seq'), 'kv'), may hold values from -6 to 6
- cond_values: bfloat16 [8, 8192, 2048], P(None, ('guide', 'seq'), 'kv'), may hold values from -6 to 6
- uncond_keys: bfloat16 [8, 2048, 2048], P(None, ('guide', 'seq'), 'kv'), may hold values from -6 to 6
- uncond_values: bfloat16 [8, 2048, 2048], P(None, ('guide', 'seq'), 'kv'), may hold values from -6 to 6
Outputs:
- mixed: float32 [8, 65536], P('guide', ('kv', 'seq'))
Inputs may be any that keep to these rules, and one draw needn't show every extreme that they name: lengths[0] lies in 1 to 8192 and some request has exactly 8192; lengths[1] lies in 1 to 2048 and some request has exactly 2048. `slot_owner`: each row is a permutation of the 8 requests. `allowed_ids`: the ids of the i-th aligned block of 1024 entries are distinct and lie in rows i * 2048 to (i + 1) * 2048 - 1 of the table.
All inputs are finite; a program needn't handle non-finite values.
Results may differ from a plain program's by a relative error of at most 0.0039.
Values may be sent and summed in bfloat16 or wider, within the bound.
A program may use at most 128 MiB of HBM per device.

v0:
```python
import jax
import jax.numpy as jnp
from jax import lax
from jax.sharding import PartitionSpec as P

D = 4608
H = 32
HD = 128
EPS = 1e-06
ATTN_CAP = 50.0
LOGIT_CAP = 30.0
THETA = 10000.0
HIGHEST = lax.Precision.HIGHEST


def rotary(values, position):
    half_size = values.shape[-1] // 2
    frequency = THETA ** (-2.0 * jnp.arange(half_size, dtype=jnp.float32) / values.shape[-1])
    angles = position[:, None, None] * frequency
    first_half = values[..., :half_size]
    second_half = values[..., half_size:]
    cosine = jnp.cos(angles)
    sine_part = jnp.sin(angles)
    return jnp.concatenate(
        [
            first_half * cosine - second_half * sine_part,
            second_half * cosine + first_half * sine_part,
        ],
        axis=-1,
    )


def to_slots(slot_pick, array):
    flat = array.astype(jnp.float32).reshape(array.shape[0], array.shape[1], -1)
    moved = jnp.einsum("gsr,gre->gse", slot_pick, flat, precision=HIGHEST)
    return moved.reshape(array.shape).astype(array.dtype)


def to_requests(slot_pick, array):
    flat = array.astype(jnp.float32).reshape(array.shape[0], array.shape[1], -1)
    moved = jnp.einsum("gsr,gse->gre", slot_pick, flat, precision=HIGHEST)
    return moved.reshape(array.shape).astype(array.dtype)


def attend_block(queries, key_block, value_block, slot_len, first_pos, tile_len):
    slot_count, block_len = (key_block.shape[0], key_block.shape[1])
    local_kv, group_size, head_size = (queries.shape[1], queries.shape[2], queries.shape[3])
    live_len = jnp.clip(jnp.max(slot_len) - first_pos, 0, block_len)
    tile_count = (live_len + tile_len - 1) // tile_len

    def one_tile(tile_index, carry):
        numer, denom = carry
        tile_start = tile_index * tile_len
        key_tile = key_block.reshape(slot_count, tile_len, local_kv, head_size)
        value_tile = value_block.reshape(slot_count, tile_len, local_kv, head_size)
        scores = jnp.einsum(
            "rkgd,rtkd->rkgt", queries, key_tile, preferred_element_type=jnp.float32
        )
        places = first_pos + tile_start + jnp.arange(tile_len, dtype=jnp.int32)
        visible = places[None, None, None, :] < slot_len[:, None, None, None]
        probs = jnp.where(visible, jnp.exp(ATTN_CAP * jnp.tanh(scores / ATTN_CAP)), 0.0)
        numer = numer + jnp.einsum(
            "rkgt,rtkd->rkgd",
            probs.astype(jnp.bfloat16),
            value_tile,
            preferred_element_type=jnp.float32,
        )
        denom = denom + jnp.sum(probs, axis=-1)
        return (numer, denom)

    start_numer = jnp.zeros((slot_count, local_kv, group_size, head_size), jnp.float32)
    start_denom = jnp.zeros((slot_count, local_kv, group_size), jnp.float32)
    return lax.fori_loop(0, tile_count, one_tile, (start_numer, start_denom))


def on_device(
    hidden,
    lengths,
    slot_owner,
    allowed_ids,
    guidance,
    pre_attn_gain,
    post_attn_gain,
    pre_ffw_gain,
    post_ffw_gain,
    final_gain,
    query_weight,
    key_weight,
    value_weight,
    output_weight,
    gate_weight,
    up_weight,
    down_weight,
    embedding,
    cond_keys,
    cond_values,
    uncond_keys,
    uncond_values,
):
    kinds, requests, width_local = hidden.shape
    stream_count = kinds * requests
    local_heads = query_weight.shape[1] // HD
    local_kv = key_weight.shape[1] // HD
    group_size = local_heads // local_kv
    streams = hidden.astype(jnp.float32)
    normed = (streams * pre_attn_gain).astype(jnp.bfloat16).reshape(stream_count, width_local)
    query_part = jnp.dot(normed, query_weight, preferred_element_type=jnp.float32)
    key_part = jnp.dot(normed, key_weight, preferred_element_type=jnp.float32)
    value_part = jnp.dot(normed, value_weight, preferred_element_type=jnp.float32)
    square_part = jnp.sum(streams * streams, axis=-1)
    square_sum, query_sum, key_sum, value_sum = lax.psum(
        (square_part, query_part, key_part, value_part), ("guide", "seq")
    )
    row_scale = lax.rsqrt(square_sum / D + EPS).reshape(stream_count, 1)
    position = lengths.astype(jnp.float32).reshape(stream_count)
    queries = (
        rotary((query_sum * row_scale).reshape(stream_count, local_heads, HD), position)
        * (D // H) ** (-0.5)
    ).astype(jnp.bfloat16)
    new_keys = rotary((key_sum * row_scale).reshape(stream_count, local_kv, HD), position).astype(
        jnp.bfloat16
    )
    new_values = (value_sum * row_scale).astype(jnp.bfloat16)
    queries = queries.reshape(kinds, requests, local_kv, group_size, HD)
    new_keys = new_keys.reshape(kinds, requests, local_kv, HD)
    new_values = new_values.reshape(kinds, requests, local_kv, HD)
    matches = slot_owner[:, :, None] == jnp.arange(requests, dtype=jnp.int32)[None, None, :]
    slot_pick = matches.astype(jnp.float32)
    slot_len = jnp.sum(jnp.where(matches, lengths[:, None, :], 0), axis=-1)
    slot_queries = to_slots(slot_pick, queries)
    slot_keys = to_slots(slot_pick, new_keys)
    slot_values = to_slots(slot_pick, new_values)
    guide_index = lax.axis_index("guide")
    seq_index = lax.axis_index("seq")
    block_index = guide_index * lax.axis_size("seq") + seq_index
    cond_len = cond_keys.shape[1]
    uncond_len = uncond_keys.shape[1]
    cond_numer, cond_denom = attend_block(
        slot_queries[0],
        cond_keys,
        cond_values,
        slot_len[0],
        block_index * cond_len,
        min(256, cond_len),
    )
    uncond_numer, uncond_denom = attend_block(
        slot_queries[1],
        uncond_keys,
        uncond_values,
        slot_len[1],
        block_index * uncond_len,
        min(256, uncond_len),
    )
    numer_part = jnp.stack([cond_numer, uncond_numer])
    denom_part = jnp.stack([cond_denom, uncond_denom])
    numer_sum, denom_sum = lax.psum((numer_part, denom_part), ("guide", "seq"))
    own_score = jnp.einsum(
        "gskjd,gskd->gskj", slot_queries, slot_keys, preferred_element_type=jnp.float32
    )
    own_prob = jnp.exp(ATTN_CAP * jnp.tanh(own_score / ATTN_CAP))
    own_weight = own_prob.astype(jnp.bfloat16).astype(jnp.float32)
    numer_total = (
        numer_sum + own_weight[..., None] * slot_values.astype(jnp.float32)[:, :, :, None, :]
    )
    denom_total = denom_sum + own_prob
    attended_slots = (numer_total / denom_total[..., None]).astype(jnp.bfloat16)
    attended = to_requests(slot_pick, attended_slots).reshape(stream_count, local_heads * HD)
    out_part = jnp.dot(attended, output_weight, preferred_element_type=jnp.float32)
    projected = lax.psum(out_part, "kv").reshape(kinds, requests, width_local)
    branch_sq = lax.psum(jnp.sum(projected * projected, axis=-1), ("guide", "seq"))
    out_scale = lax.rsqrt(branch_sq / D + EPS)
    middle = streams + projected * out_scale[..., None] * post_attn_gain
    middle_sq = lax.psum(jnp.sum(middle * middle, axis=-1), ("guide", "seq"))
    ffw_in = (middle * pre_ffw_gain).astype(jnp.bfloat16).reshape(stream_count, width_local)
    ffw_scale = lax.rsqrt(middle_sq / D + EPS).reshape(stream_count, 1)
    gate_part = jnp.dot(ffw_in, gate_weight, preferred_element_type=jnp.float32)
    upward_part = jnp.dot(ffw_in, up_weight, preferred_element_type=jnp.float32)
    gate_sum, upward_sum = lax.psum((gate_part, upward_part), ("guide", "seq"))
    activ = (jax.nn.gelu(gate_sum * ffw_scale, approximate=True) * (upward_sum * ffw_scale)).astype(
        jnp.bfloat16
    )
    down_part = jnp.dot(activ, down_weight, preferred_element_type=jnp.float32)
    ffw_out = lax.psum(down_part, "kv").reshape(kinds, requests, width_local)
    ffw_sq = lax.psum(jnp.sum(ffw_out * ffw_out, axis=-1), ("guide", "seq"))
    branch_scale = lax.rsqrt(ffw_sq / D + EPS)
    last = middle + ffw_out * branch_scale[..., None] * post_ffw_gain
    last_sq = lax.psum(jnp.sum(last * last, axis=-1), ("guide", "seq"))
    final_scale = lax.rsqrt(last_sq / D + EPS)
    final_rows = (last * final_gain).astype(jnp.bfloat16)
    half_rows = lax.all_gather(final_rows, "seq", axis=2, tiled=True)
    table_rows = embedding.shape[0]
    block_first = (lax.axis_index("kv") * lax.axis_size("seq") + seq_index) * table_rows
    picked = jnp.take(embedding, allowed_ids - block_first, axis=0)
    logit_part = jnp.einsum(
        "sd,ad->sa",
        half_rows.reshape(stream_count, half_rows.shape[2]),
        picked,
        preferred_element_type=jnp.float32,
    )
    logit_term = jnp.transpose(logit_part.reshape(kinds, requests, picked.shape[0]), (1, 0, 2))
    logit_share = lax.psum_scatter(logit_term, "guide", scatter_dimension=0, tiled=True)
    half_req = requests // 2
    first_req = guide_index * half_req
    share_scale = jnp.transpose(
        lax.dynamic_slice_in_dim(final_scale, first_req, half_req, 1), (1, 0)
    )
    capped = LOGIT_CAP * jnp.tanh(logit_share * share_scale[:, :, None] / LOGIT_CAP)
    share_weight = lax.dynamic_slice_in_dim(guidance, first_req, half_req, 0)
    return capped[:, 1] + share_weight[:, None] * (capped[:, 0] - capped[:, 1])


def solution(mesh):
    return jax.shard_map(
        on_device,
        mesh=mesh,
        in_specs=(
            P(None, None, ("guide", "seq")),
            P(),
            P(),
            P(("kv", "seq")),
            P(),
            P(("guide", "seq")),
            P(("guide", "seq")),
            P(("guide", "seq")),
            P(("guide", "seq")),
            P(("guide", "seq")),
            P(("guide", "seq"), "kv"),
            P(("guide", "seq"), "kv"),
            P(("guide", "seq"), "kv"),
            P("kv", ("guide", "seq")),
            P(("guide", "seq"), "kv"),
            P(("guide", "seq"), "kv"),
            P("kv", ("guide", "seq")),
            P(("kv", "seq"), "guide"),
            P(None, ("guide", "seq"), "kv"),
            P(None, ("guide", "seq"), "kv"),
            P(None, ("guide", "seq"), "kv"),
            P(None, ("guide", "seq"), "kv"),
        ),
        out_specs=P("guide", ("kv", "seq")),
        check_vma=False,
    )
```

profile of v0, /device:TPU:1, one launch (start us, length us, event | category | flops | bytes accessed | tf_op | source)
XLA Modules:
  0.0 685.3 jit_solution(3180978337750881133)
XLA Ops:
  6.5 1.9 fusion.79
  11.5 70.0 %psum.99 = f32[2,8]{1,0:T(2,128)S(1)} all-reduce(f32[2,8]{1,0:T(2,128)S(1)} %fusion.58), channel_id=1, replica_groups=mesh['guide'=2,'kv'=4,'seq'=16] {'guide','seq'}, use_global_device_ids=true, to_apply=%region_4.0 | all-reduce | flops 16 | bytes 128 | tf_op jit(solution)/shard_map/psum | solution.py:111
  81.6 1.7 fusion.75
  83.3 1.7 fusion.77
  86.5 23.5 %all-reduce.9.cloned.1.call-done = f32[16,1024]{1,0:T(8,128)} async-done(((f32[16,1024]{1,0:T(8,128)}), f32[16,1024]{1,0:T(8,128)}) %all-reduce.9.cloned.1.call-update) | async-done | bytes 65552 | tf_op jit(solution)/shard_map/psum | solution.py:111
  110.0 0.9 multiply_bitcast_fusion
  111.1 0.9 convolution_convert_fusion.1
  112.0 2.2 fusion.17
  114.3 2.3 while.28
  114.4 2.0 fusion.127
  116.7 1.4 fusion.39
  118.2 1.6 while.29
  118.3 1.3 convolution_add_fusion.2
  121.3 95.4 %all-reduce.15.cloned.1.call-done = (f32[2,8,4,2]{1,2,3,0:T(4,128)}, f32[16,512]{1,0:T(8,128)}, f32[16,512]{1,0:T(8,128)}) async-done(((f32[2,8,4,2]{1,2,3,0:T(4,128)}, f32[16,512]{1,0:T(8,128)}, f32[16,512]{1,0:T(8,128)}), (f32[2,8,4,2]{1,2,3,0:T(4,128)}, f32[16,512]{1,0:T(8,128)}, f32[16,512]{1,0:T(8,128)})) %all-reduce.15.cloned.1.call-update) | async-done | bytes 66064 | tf_op jit(solution)/shard_map/psum | solution.py:156
  216.7 0.8 broadcast_multiply_fusion
  218.3 1.0 fusion.29
  220.3 93.1 %all-reduce.11.cloned.1.call-done = f32[2,8,4,2,128]{4,3,2,1,0:T(2,128)} async-done(((f32[2,8,4,2,128]{4,3,2,1,0:T(2,128)}), f32[2,8,4,2,128]{4,3,2,1,0:T(2,128)}) %all-reduce.11.cloned.1.call-update) | async-done | bytes 65552 | tf_op jit(solution)/shard_map/psum | solution.py:156
  313.4 1.0 fusion.50
  314.8 13.2 %psum.104 = f32[16,144]{1,0:T(8,128)S(1)} all-reduce(f32[16,144]{1,0:T(8,128)S(1)} %fusion.99), channel_id=1, replica_groups=mesh['guide'=2,'kv'=4,'seq'=16] {'kv'}, use_global_device_ids=true, to_apply=%region_16.17 | all-reduce | flops 2304 | bytes 18432 | tf_op jit(solution)/shard_map/psum | solution.py:169
  328.1 67.2 %psum.105 = f32[2,8]{1,0:T(2,128)S(1)} all-reduce(f32[2,8]{1,0:T(2,128)S(1)} %reduce_sum.83), channel_id=1, replica_groups=mesh['guide'=2,'kv'=4,'seq'=16] {'guide','seq'}, use_global_device_ids=true, to_apply=%region_18.19 | all-reduce | flops 16 | bytes 128 | tf_op jit(solution)/shard_map/psum | solution.py:170
  395.5 1.3 fusion.89
  397.3 1.3 fusion.91
  398.7 14.8 %gather_fusion = bf16[1024,2304]{1,0:T(8,128)(2,1)} fusion(bf16[2048,2304]{1,0:T(8,128)(2,1)} %param.43, s32[1024]{0:T(1024)S(1)} %fusion.88), kind=kCustom, calls=%fused_computation | custom fusion | bytes 9441280 | tf_op jit(solution)/shard_map/jit(_take)/gather | solution.py:193
  414.7 62.7 %psum.107 = f32[2,8]{1,0:T(2,128)S(1)} all-reduce(f32[2,8]{1,0:T(2,128)S(1)} %get-tuple-element.260), channel_id=1, replica_groups=mesh['guide'=2,'kv'=4,'seq'=16] {'guide','seq'}, use_global_device_ids=true, to_apply=%region_21.22 | all-reduce | flops 16 | bytes 128 | tf_op jit(solution)/shard_map/psum | solution.py:173
  477.5 21.1 %all-reduce.17.cloned.1.call-done = (f32[16,9216]{1,0:T(8,128)}, f32[16,9216]{1,0:T(8,128)}) async-done(((f32[16,9216]{1,0:T(8,128)}, f32[16,9216]{1,0:T(8,128)}), (f32[16,9216]{1,0:T(8,128)}, f32[16,9216]{1,0:T(8,128)})) %all-reduce.17.cloned.1.call-update) | async-done | bytes 1179664 | tf_op jit(solution)/shard_map/psum | solution.py:178
  498.6 3.0 fusion.42
  501.6 13.1 %psum.109 = f32[16,144]{1,0:T(8,128)S(1)} all-reduce(f32[16,144]{1,0:T(8,128)S(1)} %fusion.42), channel_id=1, replica_groups=mesh['guide'=2,'kv'=4,'seq'=16] {'kv'}, use_global_device_ids=true, to_apply=%region_23.24 | all-reduce | flops 2304 | bytes 18432 | tf_op jit(solution)/shard_map/psum | solution.py:183
  515.0 69.8 %psum.110 = f32[2,8]{1,0:T(2,128)S(1)} all-reduce(f32[2,8]{1,0:T(2,128)S(1)} %reduce_sum.86), channel_id=1, replica_groups=mesh['guide'=2,'kv'=4,'seq'=16] {'guide','seq'}, use_global_device_ids=true, to_apply=%region_25.26 | all-reduce | flops 16 | bytes 128 | tf_op jit(solution)/shard_map/psum | solution.py:184
  585.1 18.4 %all_gather.3 = bf16[2,8,2304]{1,0,2:T(2,128)(2,1)S(1)} all-gather(bf16[2,8,144]{1,0,2:T(2,128)(2,1)S(1)} %copy.69), channel_id=1, replica_groups=mesh['guide'=2,'kv'=4,'seq'=16] {'seq'}, dimensions={2}, use_global_device_ids=true | all-gather | bytes 78336 | tf_op jit(solution)/shard_map/all_gather | solution.py:190
  603.5 4.7 fusion.21
  608.3 68.8 %psum.111 = f32[2,8]{1,0:T(2,128)S(1)} all-reduce(f32[2,8]{1,0:T(2,128)S(1)} %get-tuple-element.266), channel_id=1, replica_groups=mesh['guide'=2,'kv'=4,'seq'=16] {'guide','seq'}, use_global_device_ids=true, to_apply=%region_28.29 | all-reduce | flops 16 | bytes 128 | tf_op jit(solution)/shard_map/psum | solution.py:187
  677.1 0.9 fusion.53
  (97 shorter events, 10.7 us)
Async XLA Ops:
  6.5 389.0 %copy-start = (bf16[144,9216]{1,0:T(8,128)(2,1)S(1)}, bf16[144,9216]{1,0:T(8,128)(2,1)}, u32[]{:S(2)}) copy-start(bf16[144,9216]{1,0:T(8,128)(2,1)} %param.41) | copy-start | bytes 7962628
  6.5 103.4 %all-reduce.9.cloned.1.call-start = ((), (), s32[]{:S(2)}) async-start(), calls=%async_computation | async-start | bytes 131072 | tf_op jit(solution)/shard_map/psum | solution.py:111
  8.5 208.2 %all-reduce.15.cloned.1.call-start = ((), (), s32[]{:S(2)}) async-start(), calls=%async_computation.3 | async-start | bytes 147456 | tf_op jit(solution)/shard_map/psum | solution.py:156
  118.1 99.7 %copy-start.4 = (s32[2,8]{1,0:T(2,128)S(1)}, s32[2,8]{1,0:T(2,128)}, u32[]{:S(2)}) copy-start(s32[2,8]{1,0:T(2,128)} %param.28) | copy-start | bytes 196
  118.1 196.5 %copy-start.2 = (bf16[1024,144]{0,1:T(8,128)(2,1)S(1)}, bf16[1024,144]{0,1:T(8,128)(2,1)}, u32[]{:S(2)}) copy-start(bf16[1024,144]{0,1:T(8,128)(2,1)} %param.39) | copy-start | bytes 884740
  118.1 277.2 %copy-start.3 = (bf16[2,8,144]{2,1,0:T(8,128)(2,1)S(1)}, bf16[2,8,144]{2,1,0:T(8,128)(2,1)}, u32[]{:S(2)}) copy-start(bf16[2,8,144]{2,1,0:T(8,128)(2,1)} %param.26) | copy-start | bytes 13828
  118.2 277.2 %copy-start.7 = (f32[144]{0:T(256)S(1)}, f32[144]{0:T(256)}, u32[]{:S(2)}) copy-start(f32[144]{0:T(256)} %param.32) | copy-start | bytes 1732
  118.2 277.4 %copy-start.6 = (f32[144]{0:T(256)S(1)}, f32[144]{0:T(256)}, u32[]{:S(2)}) copy-start(f32[144]{0:T(256)} %param.33) | copy-start | bytes 1732
  120.5 192.9 %all-reduce.11.cloned.1.call-start = ((), (), s32[]{:S(2)}) async-start(), calls=%async_computation.1 | async-start | bytes 131072 | tf_op jit(solution)/shard_map/psum | solution.py:156
  121.3 377.4 %all-reduce.17.cloned.1.call-start = ((), (), s32[]{:S(2)}) async-start(), calls=%async_computation.4 | async-start | bytes 2359296 | tf_op jit(solution)/shard_map/psum | solution.py:178
  395.3 2.0 copy-start.1
  397.3 1.4 copy-start.5
  398.6 278.5 %all-reduce.13.cloned.1.call-start = ((), (), s32[]{:S(2)}) async-start(), calls=%async_computation.2 | async-start | bytes 131072
  398.7 14.8 %copy-start.11 = (u32[128]{0:T(128)S(1)}, u32[128]{0:T(128)}, u32[]{:S(2)}) copy-start(u32[128]{0:T(128)} %constant.168) | copy-start | bytes 1540
  413.5 101.5 %copy-start.10 = (f32[8]{0:T(128)S(1)}, f32[8]{0:T(128)}, u32[]{:S(2)}) copy-start(f32[8]{0:T(128)} %param.30) | copy-start | bytes 100
  413.5 171.4 %copy-start.8 = (f32[144]{0:T(256)S(1)}, f32[144]{0:T(256)}, u32[]{:S(2)}) copy-start(f32[144]{0:T(256)} %param.34) | copy-start | bytes 1732
  413.5 171.4 %copy-start.9 = (f32[144]{0:T(256)S(1)}, f32[144]{0:T(256)}, u32[]{:S(2)}) copy-start(f32[144]{0:T(256)} %param.35) | copy-start | bytes 1732
Sparse Core Ops, SparseCore 0:
  10.6 99.2 all-reduce.8
  120.6 96.0 all-reduce.14
  220.0 93.3 all-reduce.10
  398.7 99.8 all-reduce.16
  608.4 23.3 all-reduce.12
where the time goes:
time: 686 us; the launch traced here: 685 us
  blocking collectives  383 us (56%)
  waiting for transfers between devices  233 us (34%)
  matrix products  25 us (4%)
  local copies, waits for them, and re-layouts  17.3 us (3%)
  between operations  15.4 us (2%)
  other arithmetic  10.9 us (2%)
    psum x2, waiting for transfers between devices, on_device(): numer_sum, denom_sum = lax.psum((numer_part, denom_part), ('guide', 'seq'))  189 us
    psum x1, blocking collectives, on_device(): lax.psum((square_part, query_part, key_part, value_part), ('guide', 'seq'))  70 us
    psum x1, blocking collectives, on_device(): ffw_sq = lax.psum(jnp.sum(ffw_out * ffw_out, axis=-1), ('guide', 'seq'))  69.8 us
    psum x1, blocking collectives, on_device(): last_sq = lax.psum(jnp.sum(last * last, axis=-1), ('guide', 'seq'))  68.8 us
    psum x1, blocking collectives, on_device(): lax.psum(jnp.sum(projected * projected, axis=-1), ('guide', 'seq'))  67.2 us
    psum x1, blocking collectives, on_device(): middle_sq = lax.psum(jnp.sum(middle * middle, axis=-1), ('guide', 'seq'))  62.7 us
    psum x1, waiting for transfers between devices, on_device(): lax.psum((square_part, query_part, key_part, value_part), ('guide', 'seq'))  23.5 us
    psum x1, waiting for transfers between devices, on_device(): gate_sum, upward_sum = lax.psum((gate_part, upward_part), ('guide', 'seq'))  21.1 us
  transfers between devices with their start and end apart: 5, of which 4 were waited for; matrix products, arithmetic and copies ran while one was open for 4% of the time, Pallas kernels for 0%

commit v1 on v0

--- a/solution.py
+++ b/solution.py
@@ -181,7 +181,9 @@
     )
     down_part = jnp.dot(activ, down_weight, preferred_element_type=jnp.float32)
     ffw_out = lax.psum(down_part, "kv").reshape(kinds, requests, width_local)
-    ffw_sq = lax.psum(jnp.sum(ffw_out * ffw_out, axis=-1), ("guide", "seq"))
+    ffw_sq = jnp.sum(ffw_out * ffw_out, axis=-1)
+    for mesh_axis in ("guide", "seq"):
+        ffw_sq = lax.psum(ffw_sq, mesh_axis)
     branch_scale = lax.rsqrt(ffw_sq / D + EPS)
     last = middle + ffw_out * branch_scale[..., None] * post_ffw_gain
     last_sq = lax.psum(jnp.sum(last * last, axis=-1), ("guide", "seq"))

time: 686 us -> 662 us (0.965)
  blocking collectives: 383 us -> 359 us
    psum x1 -> x2, blocking collectives: 69.8 us -> 37.9 us  [on_device(): ffw_sq = lax.psum(ffw_sq, mesh_axis)]
    psum x1, blocking collectives: 68.8 us -> 77.5 us  [on_device(): last_sq = lax.psum(jnp.sum(last * last, axis=-1), ('guide', 'seq'))]
where the time goes in v1:
time: 662 us; the launch traced here: 661 us
  blocking collectives  359 us (54%)
  waiting for transfers between devices  233 us (35%)
  matrix products  25 us (4%)
  local copies, waits for them, and re-layouts  17.3 us (3%)
  between operations  15.4 us (2%)
  other arithmetic  10.9 us (2%)
    psum x2, waiting for transfers between devices, on_device(): numer_sum, denom_sum = lax.psum((numer_part, denom_part), ('guide', 'seq'))  189 us
    psum x1, blocking collectives, on_device(): last_sq = lax.psum(jnp.sum(last * last, axis=-1), ('guide', 'seq'))  77.5 us
    psum x1, blocking collectives, on_device(): lax.psum((square_part, query_part, key_part, value_part), ('guide', 'seq'))  70 us
    psum x1, blocking collectives, on_device(): lax.psum(jnp.sum(projected * projected, axis=-1), ('guide', 'seq'))  67.2 us
    psum x1, blocking collectives, on_device(): middle_sq = lax.psum(jnp.sum(middle * middle, axis=-1), ('guide', 'seq'))  62.7 us
    psum x2, blocking collectives, on_device(): ffw_sq = lax.psum(ffw_sq, mesh_axis)  37.9 us
    psum x1, waiting for transfers between devices, on_device(): lax.psum((square_part, query_part, key_part, value_part), ('guide', 'seq'))  23.5 us
    psum x1, waiting for transfers between devices, on_device(): gate_sum, upward_sum = lax.psum((gate_part, upward_part), ('guide', 'seq'))  21.1 us
  transfers between devices with their start and end apart: 5, of which 4 were waited for; matrix products, arithmetic and copies ran while one was open for 4% of the time, Pallas kernels for 0%

profile of v1, /device:TPU:1, one launch (start us, length us, event | category | flops | bytes accessed | tf_op | source)
XLA Modules:
  0.0 660.7 jit_solution(10040463177916243153)
XLA Ops:
  6.5 1.9 fusion.79
  11.5 70.0 %psum.106 = f32[2,8]{1,0:T(2,128)S(1)} all-reduce(f32[2,8]{1,0:T(2,128)S(1)} %fusion.58), channel_id=1, replica_groups=mesh['guide'=2,'kv'=4,'seq'=16] {'guide','seq'}, use_global_device_ids=true, to_apply=%region_4.0 | all-reduce | flops 16 | bytes 128 | tf_op jit(solution)/shard_map/psum | solution.py:111
  81.6 1.7 fusion.75
  83.3 1.7 fusion.77
  86.5 23.5 %all-reduce.9.cloned.1.call-done = f32[16,1024]{1,0:T(8,128)} async-done(((f32[16,1024]{1,0:T(8,128)}), f32[16,1024]{1,0:T(8,128)}) %all-reduce.9.cloned.1.call-update) | async-done | bytes 65552 | tf_op jit(solution)/shard_map/psum | solution.py:111
  110.0 0.9 multiply_bitcast_fusion
  111.1 0.9 convolution_convert_fusion.1
  112.0 2.2 fusion.17
  114.3 2.3 while.28
  114.4 2.0 fusion.127
  116.7 1.4 fusion.39
  118.2 1.6 while.29
  118.3 1.3 convolution_add_fusion.2
  121.3 95.4 %all-reduce.15.cloned.1.call-done = (f32[2,8,4,2]{1,2,3,0:T(4,128)}, f32[16,512]{1,0:T(8,128)}, f32[16,512]{1,0:T(8,128)}) async-done(((f32[2,8,4,2]{1,2,3,0:T(4,128)}, f32[16,512]{1,0:T(8,128)}, f32[16,512]{1,0:T(8,128)}), (f32[2,8,4,2]{1,2,3,0:T(4,128)}, f32[16,512]{1,0:T(8,128)}, f32[16,512]{1,0:T(8,128)})) %all-reduce.15.cloned.1.call-update) | async-done | bytes 66064 | tf_op jit(solution)/shard_map/psum | solution.py:156
  218.3 1.0 fusion.29
  220.3 93.1 %all-reduce.11.cloned.1.call-done = f32[2,8,4,2,128]{4,3,2,1,0:T(2,128)} async-done(((f32[2,8,4,2,128]{4,3,2,1,0:T(2,128)}), f32[2,8,4,2,128]{4,3,2,1,0:T(2,128)}) %all-reduce.11.cloned.1.call-update) | async-done | bytes 65552 | tf_op jit(solution)/shard_map/psum | solution.py:156
  313.4 1.0 fusion.50
  314.8 13.2 %psum.111 = f32[16,144]{1,0:T(8,128)S(1)} all-reduce(f32[16,144]{1,0:T(8,128)S(1)} %fusion.99), channel_id=1, replica_groups=mesh['guide'=2,'kv'=4,'seq'=16] {'kv'}, use_global_device_ids=true, to_apply=%region_16.17 | all-reduce | flops 2304 | bytes 18432 | tf_op jit(solution)/shard_map/psum | solution.py:169
  328.1 67.2 %psum.112 = f32[2,8]{1,0:T(2,128)S(1)} all-reduce(f32[2,8]{1,0:T(2,128)S(1)} %reduce_sum.83), channel_id=1, replica_groups=mesh['guide'=2,'kv'=4,'seq'=16] {'guide','seq'}, use_global_device_ids=true, to_apply=%region_18.19 | all-reduce | flops 16 | bytes 128 | tf_op jit(solution)/shard_map/psum | solution.py:170
  395.5 1.3 fusion.89
  397.3 1.3 fusion.91
  398.7 14.8 %gather_fusion = bf16[1024,2304]{1,0:T(8,128)(2,1)} fusion(bf16[2048,2304]{1,0:T(8,128)(2,1)} %param.43, s32[1024]{0:T(1024)S(1)} %fusion.88), kind=kCustom, calls=%fused_computation | custom fusion | bytes 9441280 | tf_op jit(solution)/shard_map/jit(_take)/gather | solution.py:195
  414.7 62.7 %psum.114 = f32[2,8]{1,0:T(2,128)S(1)} all-reduce(f32[2,8]{1,0:T(2,128)S(1)} %get-tuple-element.260), channel_id=1, replica_groups=mesh['guide'=2,'kv'=4,'seq'=16] {'guide','seq'}, use_global_device_ids=true, to_apply=%region_21.22 | all-reduce | flops 16 | bytes 128 | tf_op jit(solution)/shard_map/psum | solution.py:173
  477.5 21.1 %all-reduce.17.cloned.1.call-done = (f32[16,9216]{1,0:T(8,128)}, f32[16,9216]{1,0:T(8,128)}) async-done(((f32[16,9216]{1,0:T(8,128)}, f32[16,9216]{1,0:T(8,128)}), (f32[16,9216]{1,0:T(8,128)}, f32[16,9216]{1,0:T(8,128)})) %all-reduce.17.cloned.1.call-update) | async-done | bytes 1179664 | tf_op jit(solution)/shard_map/psum | solution.py:178
  498.6 3.0 fusion.42
  501.6 13.1 %psum.116 = f32[16,144]{1,0:T(8,128)S(1)} all-reduce(f32[16,144]{1,0:T(8,128)S(1)} %fusion.42), channel_id=1, replica_groups=mesh['guide'=2,'kv'=4,'seq'=16] {'kv'}, use_global_device_ids=true, to_apply=%region_23.24 | all-reduce | flops 2304 | bytes 18432 | tf_op jit(solution)/shard_map/psum | solution.py:183
  514.9 6.7 %psum.117 = f32[2,8]{1,0:T(2,128)S(1)} all-reduce(f32[2,8]{1,0:T(2,128)S(1)} %reduce_sum.86), channel_id=1, replica_groups=mesh['guide'=2,'kv'=4,'seq'=16] {'guide'}, use_global_device_ids=true, to_apply=%region_25.26 | all-reduce | flops 16 | bytes 128 | tf_op jit(solution)/shard_map/psum | solution.py:186
  521.7 31.2 %psum.118 = f32[2,8]{1,0:T(2,128)S(1)} all-reduce(f32[2,8]{1,0:T(2,128)S(1)} %psum.117), channel_id=1, replica_groups=mesh['guide'=2,'kv'=4,'seq'=16] {'seq'}, use_global_device_ids=true, to_apply=%region_26.27 | all-reduce | flops 16 | bytes 128 | tf_op jit(solution)/shard_map/psum | solution.py:186
  553.2 17.0 %all_gather.3 = bf16[2,8,2304]{1,0,2:T(2,128)(2,1)S(1)} all-gather(bf16[2,8,144]{1,0,2:T(2,128)(2,1)S(1)} %copy.69), channel_id=1, replica_groups=mesh['guide'=2,'kv'=4,'seq'=16] {'seq'}, dimensions={2}, use_global_device_ids=true | all-gather | bytes 78336 | tf_op jit(solution)/shard_map/all_gather | solution.py:192
  570.2 4.7 fusion.21
  575.0 77.5 %psum.119 = f32[2,8]{1,0:T(2,128)S(1)} all-reduce(f32[2,8]{1,0:T(2,128)S(1)} %get-tuple-element.266), channel_id=1, replica_groups=mesh['guide'=2,'kv'=4,'seq'=16] {'guide','seq'}, use_global_device_ids=true, to_apply=%region_29.30 | all-reduce | flops 16 | bytes 128 | tf_op jit(solution)/shard_map/psum | solution.py:189
  652.5 0.9 fusion.53
  (98 shorter events, 11.5 us)
Async XLA Ops:
  6.5 389.0 %copy-start = (bf16[144,9216]{1,0:T(8,128)(2,1)S(1)}, bf16[144,9216]{1,0:T(8,128)(2,1)}, u32[]{:S(2)}) copy-start(bf16[144,9216]{1,0:T(8,128)(2,1)} %param.41) | copy-start | bytes 7962628
  6.5 103.4 %all-reduce.9.cloned.1.call-start = ((), (), s32[]{:S(2)}) async-start(), calls=%async_computation | async-start | bytes 131072 | tf_op jit(solution)/shard_map/psum | solution.py:111
  8.5 208.2 %all-reduce.15.cloned.1.call-start = ((), (), s32[]{:S(2)}) async-start(), calls=%async_computation.3 | async-start | bytes 147456 | tf_op jit(solution)/shard_map/psum | solution.py:156
  118.1 99.7 %copy-start.4 = (s32[2,8]{1,0:T(2,128)S(1)}, s32[2,8]{1,0:T(2,128)}, u32[]{:S(2)}) copy-start(s32[2,8]{1,0:T(2,128)} %param.28) | copy-start | bytes 196
  118.1 196.5 %copy-start.2 = (bf16[1024,144]{0,1:T(8,128)(2,1)S(1)}, bf16[1024,144]{0,1:T(8,128)(2,1)}, u32[]{:S(2)}) copy-start(bf16[1024,144]{0,1:T(8,128)(2,1)} %param.39) | copy-start | bytes 884740
  118.1 277.2 %copy-start.3 = (bf16[2,8,144]{2,1,0:T(8,128)(2,1)S(1)}, bf16[2,8,144]{2,1,0:T(8,128)(2,1)}, u32[]{:S(2)}) copy-start(bf16[2,8,144]{2,1,0:T(8,128)(2,1)} %param.26) | copy-start | bytes 13828
  118.2 277.2 %copy-start.7 = (f32[144]{0:T(256)S(1)}, f32[144]{0:T(256)}, u32[]{:S(2)}) copy-start(f32[144]{0:T(256)} %param.32) | copy-start | bytes 1732
  118.2 277.4 %copy-start.6 = (f32[144]{0:T(256)S(1)}, f32[144]{0:T(256)}, u32[]{:S(2)}) copy-start(f32[144]{0:T(256)} %param.33) | copy-start | bytes 1732
  120.5 192.9 %all-reduce.11.cloned.1.call-start = ((), (), s32[]{:S(2)}) async-start(), calls=%async_computation.1 | async-start | bytes 131072 | tf_op jit(solution)/shard_map/psum | solution.py:156
  121.3 377.4 %all-reduce.17.cloned.1.call-start = ((), (), s32[]{:S(2)}) async-start(), calls=%async_computation.4 | async-start | bytes 2359296 | tf_op jit(solution)/shard_map/psum | solution.py:178
  395.3 2.0 copy-start.1
  397.3 1.4 copy-start.5
  398.6 253.9 %all-reduce.13.cloned.1.call-start = ((), (), s32[]{:S(2)}) async-start(), calls=%async_computation.2 | async-start | bytes 131072
  398.7 14.8 %copy-start.11 = (u32[128]{0:T(128)S(1)}, u32[128]{0:T(128)}, u32[]{:S(2)}) copy-start(u32[128]{0:T(128)} %constant.168) | copy-start | bytes 1540
  413.5 108.1 %copy-start.10 = (f32[8]{0:T(128)S(1)}, f32[8]{0:T(128)}, u32[]{:S(2)}) copy-start(f32[8]{0:T(128)} %param.30) | copy-start | bytes 100
  413.5 139.4 %copy-start.8 = (f32[144]{0:T(256)S(1)}, f32[144]{0:T(256)}, u32[]{:S(2)}) copy-start(f32[144]{0:T(256)} %param.34) | copy-start | bytes 1732
  413.5 139.4 %copy-start.9 = (f32[144]{0:T(256)S(1)}, f32[144]{0:T(256)}, u32[]{:S(2)}) copy-start(f32[144]{0:T(256)} %param.35) | copy-start | bytes 1732
Sparse Core Ops, SparseCore 0:
  10.6 99.2 all-reduce.8
  120.6 96.0 all-reduce.14
  220.0 93.3 all-reduce.10
  398.7 99.8 all-reduce.16
  575.1 32.9 all-reduce.12
